TPU v7x, 32 devices: a whole 2x2x4 slice. The times are simulated.
32 devices in a mesh: blk: 4 (over z), grp: 8 (over y, x, core).
Axes of the slice: x: 2, y: 2, z: 4, core: 2. Of those that a mesh axis runs over, the one named last changes fastest.
Arguments:
- basis: bfloat16 [8, 512, 1152], P('grp', 'blk'), may hold values from -6 to 6
- coeffs: bfloat16 [2, 1152, 768], replicated, may hold values from -0.1875 to 0.1875
- stiff_blocks: bfloat16 [8, 4, 4, 128, 128], P('grp', 'blk'), as said below
- mass_blocks: bfloat16 [8, 4, 4, 128, 128], P('grp', 'blk'), as said below
- block_cols: int32 [8, 4, 4], P('grp', 'blk'), may hold values from 0 to 3
Outputs:
- basis_out: bfloat16 [8, 512, 1152], P('grp', 'blk')
- ritz_value: float32 [384], replicated
- gram: float32 [1152, 2, 1152], P('grp', None, 'blk')
Inputs may be any that keep to these rules, and one draw needn't show every extreme that they name: block_cols names row blocks of the same substructure. `mass_blocks`: real-valued blocks of order 1 / sqrt(512). `stiff_blocks`: real-valued blocks, of larger size than the mass blocks.
All inputs are finite; a program needn't handle non-finite values.
Results may differ from a plain program's by a relative error of at most 0.02.
Values may be sent and summed in bfloat16 or wider, within the bound.
No kernel may reach another device: no remote copies, remote signals or barrier semaphores. Data moves between devices by JAX's collectives and lax.ppermute only.
A program may use at most 64 MiB of HBM per device.

v0:
```python
import jax
import jax.numpy as jnp
from jax import lax
from jax.sharding import PartitionSpec as P

epsilon = 1e-06


def apply_pair(stiff, mass, cols, field, final):
    columns = field.shape[1]
    block_rows, slots = cols.shape
    edge = stiff.shape[-1]
    own_blocks = field.reshape(block_rows, edge, columns)
    wanted = cols.reshape(-1)

    def take_blocks(arrived):
        arrived_count = arrived.shape[0]
        ident = jnp.arange(arrived_count, dtype=jnp.int32)
        selector = (wanted[:, None] == ident[None, :]).astype(jnp.bfloat16)
        taken = jnp.dot(
            selector, arrived.reshape(arrived_count, -1), preferred_element_type=jnp.float32
        )
        return taken.astype(jnp.bfloat16)

    if final:
        gathered = take_blocks(lax.all_gather(own_blocks, "blk", axis=0, tiled=True))
    else:
        gathered = take_blocks(lax.all_gather(own_blocks, "blk", axis=0, tiled=True))
    gathered = gathered.reshape(block_rows, slots, edge, columns)
    contract = (((1, 3), (1, 2)), ((0,), (0,)))
    stiff_out = lax.dot_general(stiff, gathered, contract, preferred_element_type=jnp.float32)
    mass_out = lax.dot_general(mass, gathered, contract, preferred_element_type=jnp.float32)
    return (
        stiff_out.reshape(block_rows * edge, columns),
        mass_out.reshape(block_rows * edge, columns),
    )


def body(basis, coeffs, stiff_blocks, mass_blocks, block_cols):
    stiff = stiff_blocks[0]
    mass = mass_blocks[0]
    cols = block_cols[0]
    current = basis[0]
    rows_here, columns = current.shape
    mode_count = columns // 3
    total_rows = rows_here * lax.axis_size("blk") * lax.axis_size("grp")
    for sweep in range(coeffs.shape[0]):
        turned = jnp.dot(current, coeffs[sweep], preferred_element_type=jnp.float32).astype(
            jnp.bfloat16
        )
        next_modes = turned[:, :mode_count]
        next_history = turned[:, mode_count:]
        stiff_x, mass_x = apply_pair(stiff, mass, cols, next_modes, False)
        numerator, denominator = lax.psum(
            (jnp.sum(stiff_x * mass_x, axis=0), jnp.sum(mass_x * mass_x, axis=0)), ("blk", "grp")
        )
        ritz_value = numerator / (denominator + epsilon)
        residual = stiff_x - ritz_value * mass_x
        resid_sum = lax.psum(jnp.sum(residual * residual, axis=0), ("blk", "grp"))
        next_search = (residual * lax.rsqrt(resid_sum / total_rows + epsilon)).astype(jnp.bfloat16)
        current = jnp.concatenate([next_modes, next_search, next_history], axis=1)
    stiff_rest, mass_rest = apply_pair(stiff, mass, cols, current[:, mode_count:], True)
    stiff_all = jnp.concatenate(
        [stiff_x.astype(jnp.bfloat16), stiff_rest.astype(jnp.bfloat16)], axis=1
    )
    mass_all = jnp.concatenate(
        [mass_x.astype(jnp.bfloat16), mass_rest.astype(jnp.bfloat16)], axis=1
    )
    inner = (((0,), (0,)), ((), ()))
    gram_stiff = lax.dot_general(current, stiff_all, inner, preferred_element_type=jnp.float32)
    gram_mass = lax.dot_general(current, mass_all, inner, preferred_element_type=jnp.float32)
    by_group = lax.psum_scatter(
        jnp.stack([gram_stiff, gram_mass], axis=1).astype(jnp.bfloat16),
        "grp",
        scatter_dimension=0,
        tiled=True,
    )
    gram = lax.psum_scatter(by_group, "blk", scatter_dimension=2, tiled=True).astype(jnp.float32)
    return (current[None], ritz_value, gram)


def solution(mesh):
    in_specs = (
        P("grp", "blk", None),
        P(),
        P("grp", "blk", None, None, None),
        P("grp", "blk", None, None, None),
        P("grp", "blk", None),
    )
    out_specs = (P("grp", "blk", None), P(), P("grp", None, "blk"))
    return jax.shard_map(body, mesh=mesh, in_specs=in_specs, out_specs=out_specs, check_vma=False)
```

profile of v0, /device:TPU:0, one launch (start us, length us, event | category | flops | bytes accessed | tf_op | source)
XLA Modules:
  0.0 328.8 jit_solution(17541428477707894250)
XLA Ops:
  7.3 0.9 copy-done
  8.1 1.9 fusion.8
  10.1 16.2 %all-gather = bf16[512,384]{1,0:T(8,128)(2,1)S(1)} all-gather(bf16[128,384]{1,0:T(8,128)(2,1)S(1)} %get-tuple-element.22), channel_id=2, replica_groups=mesh['blk'=4,'grp'=8] {'blk'}, dimensions={0}, use_global_device_ids=true | all-gather | bytes 491520 | tf_op jit(solution)/shard_map/all_gather | solution.py:28
  27.4 40.9 %all-reduce.1 = (f32[384]{0:T(512)S(1)}, f32[384]{0:T(512)S(1)}) all-reduce(f32[384]{0:T(512)S(1)} %get-tuple-element.12, f32[384]{0:T(512)S(1)} %get-tuple-element.11), channel_id=1, replica_groups=mesh['blk'=4,'grp'=8] {'blk','grp'}, use_global_device_ids=true, to_apply=%region_1.0 | all-reduce | flops 768 | bytes 6144 | tf_op jit(solution)/shard_map/psum | solution.py:54
  68.3 40.3 %psum.44 = f32[384]{0:T(512)S(1)} all-reduce(f32[384]{0:T(512)S(1)} %multiply_reduce_fusion.3), channel_id=1, replica_groups=mesh['blk'=4,'grp'=8] {'blk','grp'}, use_global_device_ids=true, to_apply=%region_5.0 | all-reduce | flops 384 | bytes 3072 | tf_op jit(solution)/shard_map/psum | solution.py:59
  108.7 1.9 fusion.11
  110.6 14.9 %all-gather.1 = bf16[512,384]{1,0:T(8,128)(2,1)S(1)} all-gather(bf16[128,384]{1,0:T(8,128)(2,1)S(1)} %get-tuple-element.20), channel_id=3, replica_groups=mesh['blk'=4,'grp'=8] {'blk'}, dimensions={0}, use_global_device_ids=true | all-gather | bytes 491520 | tf_op jit(solution)/shard_map/all_gather | solution.py:28
  126.6 39.9 %all-reduce = (f32[384]{0:T(512)S(1)}, f32[384]{0:T(512)S(1)}) all-reduce(f32[384]{0:T(512)S(1)} %get-tuple-element.10, f32[384]{0:T(512)S(1)} %get-tuple-element.9), channel_id=1, replica_groups=mesh['blk'=4,'grp'=8] {'blk','grp'}, use_global_device_ids=true, to_apply=%region_7.0 | all-reduce | flops 768 | bytes 6144 | tf_op jit(solution)/shard_map/psum | solution.py:54
  166.5 40.4 %psum.47 = f32[384]{0:T(512)S(1)} all-reduce(f32[384]{0:T(512)S(1)} %multiply_reduce_fusion), channel_id=1, replica_groups=mesh['blk'=4,'grp'=8] {'blk','grp'}, use_global_device_ids=true, to_apply=%region_11.0 | all-reduce | flops 384 | bytes 3072 | tf_op jit(solution)/shard_map/psum | solution.py:59
  207.0 18.3 %all-gather.2 = bf16[512,768]{1,0:T(8,128)(2,1)S(1)} all-gather(bf16[128,768]{1,0:T(8,128)(2,1)S(1)} %pad_maximum_fusion.2), channel_id=4, replica_groups=mesh['blk'=4,'grp'=8] {'blk'}, dimensions={0}, use_global_device_ids=true | all-gather | bytes 983040 | tf_op jit(solution)/shard_map/all_gather | solution.py:26
  225.3 0.6 reshape.93
  225.9 0.6 convolution_convert_fusion
  226.5 0.4 fusion.16
  226.9 0.4 fusion.17
  227.6 0.9 fusion
  228.5 0.9 fusion.1
  229.4 2.8 pad_maximum_fusion
  232.3 57.6 %reduce-scatter.5.cloned.1.call-done = bf16[144,2,1152]{2,0,1:T(8,128)(2,1)} async-done(((bf16[1152,2,1152]{2,0,1:T(8,128)(2,1)}), bf16[144,2,1152]{2,0,1:T(8,128)(2,1)}) %reduce-scatter.5.cloned.1.call-update) | async-done | bytes 663568 | tf_op jit(solution)/shard_map/reduce_scatter | solution.py:72
  289.9 3.5 %copy.28 = bf16[144,2,1152]{0,1,2:T(2,128)(2,1)S(1)} copy(bf16[144,2,1152]{2,0,1:T(8,128)(2,1)} %reduce-scatter.5.cloned.1.call-done) | data formatting | bytes 1327104
  293.4 1.5 reshape.107
  295.0 0.7 fusion.54
  295.7 24.0 %reduce-scatter.7.cloned.1.call-done = bf16[288,288]{1,0:T(8,128)(2,1)} async-done(((bf16[1152,288]{1,0:T(8,128)(2,1)}), bf16[288,288]{1,0:T(8,128)(2,1)}) %reduce-scatter.7.cloned.1.call-update) | async-done | bytes 165904
  319.7 1.1 reshape.108
  321.0 0.9 copy.21
  (35 shorter events, 3.0 us)
Async XLA Ops:
  7.2 1.0 copy-start
  7.2 19.3 %copy-start.4 = (s32[1,1,4]{2,1,0:T(1,128)S(1)}, s32[1,1,4]{2,1,0:T(1,128)}, u32[]{:S(2)}) copy-start(s32[1,1,4]{2,1,0:T(1,128)} %param.9) | copy-start | bytes 52
  7.2 19.7 %copy-start.2 = (bf16[1,1,4,128,128]{4,3,2,1,0:T(8,128)(2,1)S(1)}, bf16[1,1,4,128,128]{4,3,2,1,0:T(8,128)(2,1)}, u32[]{:S(2)}) copy-start(bf16[1,1,4,128,128]{4,3,2,1,0:T(8,128)(2,1)} %param.7) | copy-start | bytes 393220
  7.2 19.9 %copy-start.1 = (bf16[1,1,4,128,128]{4,3,2,1,0:T(8,128)(2,1)S(1)}, bf16[1,1,4,128,128]{4,3,2,1,0:T(8,128)(2,1)}, u32[]{:S(2)}) copy-start(bf16[1,1,4,128,128]{4,3,2,1,0:T(8,128)(2,1)} %param.8) | copy-start | bytes 393220
  7.2 282.7 %reduce-scatter.5.cloned.1.call-start = ((), (), s32[]{:S(2)}) async-start(), calls=%async_computation.2 | async-start | bytes 5971968 | tf_op jit(solution)/shard_map/reduce_scatter | solution.py:72
  166.5 60.0 %copy-start.3 = (f32[384]{0:T(512)}, f32[384]{0:T(512)S(1)}, u32[]{:S(2)}) copy-start(f32[384]{0:T(512)S(1)} %add_divide_fusion) | copy-start | bytes 4612
  232.3 87.4 %reduce-scatter.7.cloned.1.call-start = ((), (), s32[]{:S(2)}) async-start(), calls=%async_computation.3 | async-start | bytes 1105920
Sparse Core Ops, SparseCore 0:
  232.4 57.4 reduce-scatter.4
  295.1 24.5 reduce-scatter.6
where the time goes:
time: 330 us; the launch traced here: 329 us
  blocking collectives  211 us (64%)
  waiting for transfers between devices  81.6 us (25%)
  between operations  14.3 us (4%)
  local copies, waits for them, and re-layouts  9.36 us (3%)
  matrix products  8.84 us (3%)
  other arithmetic  3.82 us (1%)
    psum x2, blocking collectives, body(): lax.psum((jnp.sum(stiff_x * mass_x, axis=0), jnp.sum(mass_x * mass_x, axi...  80.8 us
    psum x2, blocking collectives, body(): resid_sum = lax.psum(jnp.sum(residual * residual, axis=0), ('blk', 'grp'))  80.7 us
    reduce_scatter x1, waiting for transfers between devices, body(): lax.psum_scatter(jnp.stack([gram_stiff, gram_mass], axis=1).astype(jnp.bf...  57.6 us
    all_gather x3, blocking collectives, apply_pair(): lax.all_gather(own_blocks, 'blk', axis=0, tiled=True)  49.4 us
    unnamed x3, waiting for transfers between devices  24 us
    unnamed x15, local copies, waits for them, and re-layouts  8.2 us
  transfers between devices with their start and end apart: 2, of which 2 were waited for; matrix products, arithmetic and copies ran while one was open for 0% of the time, Pallas kernels for 0%

commit v1 on v0

--- a/solution.py
+++ b/solution.py
@@ -56,7 +56,7 @@
         )
         ritz_value = numerator / (denominator + epsilon)
         residual = stiff_x - ritz_value * mass_x
-        resid_sum = lax.psum(jnp.sum(residual * residual, axis=0), ("blk", "grp"))
+        resid_sum = lax.psum(lax.psum(jnp.sum(residual * residual, axis=0), "grp"), "blk")
         next_search = (residual * lax.rsqrt(resid_sum / total_rows + epsilon)).astype(jnp.bfloat16)
         current = jnp.concatenate([next_modes, next_search, next_history], axis=1)
     stiff_rest, mass_rest = apply_pair(stiff, mass, cols, current[:, mode_count:], True)

time: 330 us -> 288 us (0.87)
  blocking collectives: 211 us -> 171 us
    psum x2 -> x4, blocking collectives: 80.7 us -> 46 us  [the longest x2 25.4 us: body(): lax.psum(jnp.sum(residual * residual, axis=0), 'grp')]
where the time goes in v1:
time: 288 us
  blocking collectives  171 us (59%)
  waiting for transfers between devices  79.8 us (28%)
  between operations  14.3 us (5%)
  local copies, waits for them, and re-layouts  9.37 us (3%)
  matrix products  8.84 us (3%)
  other arithmetic  3.83 us (1%)
    psum x2, blocking collectives, body(): lax.psum((jnp.sum(stiff_x * mass_x, axis=0), jnp.sum(mass_x * mass_x, axi...  78.6 us
    reduce_scatter x1, waiting for transfers between devices, body(): lax.psum_scatter(jnp.stack([gram_stiff, gram_mass], axis=1).astype(jnp.bf...  55.7 us
    all_gather x3, blocking collectives, apply_pair(): lax.all_gather(own_blocks, 'blk', axis=0, tiled=True)  46.9 us
    psum x2, blocking collectives, body(): lax.psum(jnp.sum(residual * residual, axis=0), 'grp')  25.4 us
    unnamed x3, waiting for transfers between devices  24 us
    psum x2, blocking collectives, body(): lax.psum(lax.psum(jnp.sum(residual * residual, axis=0), 'grp'), 'blk')  20.6 us
    unnamed x15, local copies, waits for them, and re-layouts  8.2 us
  transfers between devices with their start and end apart: 2, of which 2 were waited for; matrix products, arithmetic and copies ran while one was open for 0% of the time, Pallas kernels for 0%

profile of v1, /device:TPU:0, one launch (start us, length us, event | category | flops | bytes accessed | tf_op | source)
XLA Modules:
  0.0 287.6 jit_solution(11074586643223772297)
XLA Ops:
  7.3 0.9 copy-done
  8.1 1.9 fusion.8
  10.1 16.2 %all-gather = bf16[512,384]{1,0:T(8,128)(2,1)S(1)} all-gather(bf16[128,384]{1,0:T(8,128)(2,1)S(1)} %get-tuple-element.22), channel_id=2, replica_groups=mesh['blk'=4,'grp'=8] {'blk'}, dimensions={0}, use_global_device_ids=true | all-gather | bytes 491520 | tf_op jit(solution)/shard_map/all_gather | solution.py:28
  27.4 40.9 %all-reduce.1 = (f32[384]{0:T(512)S(1)}, f32[384]{0:T(512)S(1)}) all-reduce(f32[384]{0:T(512)S(1)} %get-tuple-element.12, f32[384]{0:T(512)S(1)} %get-tuple-element.11), channel_id=1, replica_groups=mesh['blk'=4,'grp'=8] {'blk','grp'}, use_global_device_ids=true, to_apply=%region_1.0 | all-reduce | flops 768 | bytes 6144 | tf_op jit(solution)/shard_map/psum | solution.py:54
  68.3 12.7 %psum.58 = f32[384]{0:T(512)S(1)} all-reduce(f32[384]{0:T(512)S(1)} %multiply_reduce_fusion.3), channel_id=1, replica_groups=mesh['blk'=4,'grp'=8] {'grp'}, use_global_device_ids=true, to_apply=%region_5.0 | all-reduce | flops 384 | bytes 3072 | tf_op jit(solution)/shard_map/psum | solution.py:59
  81.0 10.0 %psum.59 = f32[384]{0:T(512)S(1)} all-reduce(f32[384]{0:T(512)S(1)} %psum.58), channel_id=1, replica_groups=mesh['blk'=4,'grp'=8] {'blk'}, use_global_device_ids=true, to_apply=%region_6.0 | all-reduce | flops 384 | bytes 3072 | tf_op jit(solution)/shard_map/psum | solution.py:59
  91.1 1.9 fusion.11
  93.1 14.2 %all-gather.1 = bf16[512,384]{1,0:T(8,128)(2,1)S(1)} all-gather(bf16[128,384]{1,0:T(8,128)(2,1)S(1)} %get-tuple-element.20), channel_id=3, replica_groups=mesh['blk'=4,'grp'=8] {'blk'}, dimensions={0}, use_global_device_ids=true | all-gather | bytes 491520 | tf_op jit(solution)/shard_map/all_gather | solution.py:28
  108.4 37.7 %all-reduce = (f32[384]{0:T(512)S(1)}, f32[384]{0:T(512)S(1)}) all-reduce(f32[384]{0:T(512)S(1)} %get-tuple-element.10, f32[384]{0:T(512)S(1)} %get-tuple-element.9), channel_id=1, replica_groups=mesh['blk'=4,'grp'=8] {'blk','grp'}, use_global_device_ids=true, to_apply=%region_8.0 | all-reduce | flops 768 | bytes 6144 | tf_op jit(solution)/shard_map/psum | solution.py:54
  146.1 12.7 %psum.62 = f32[384]{0:T(512)S(1)} all-reduce(f32[384]{0:T(512)S(1)} %multiply_reduce_fusion), channel_id=1, replica_groups=mesh['blk'=4,'grp'=8] {'grp'}, use_global_device_ids=true, to_apply=%region_12.0 | all-reduce | flops 384 | bytes 3072 | tf_op jit(solution)/shard_map/psum | solution.py:59
  158.8 10.6 %psum.63 = f32[384]{0:T(512)S(1)} all-reduce(f32[384]{0:T(512)S(1)} %psum.62), channel_id=1, replica_groups=mesh['blk'=4,'grp'=8] {'blk'}, use_global_device_ids=true, to_apply=%region_13.0 | all-reduce | flops 384 | bytes 3072 | tf_op jit(solution)/shard_map/psum | solution.py:59
  169.5 16.5 %all-gather.2 = bf16[512,768]{1,0:T(8,128)(2,1)S(1)} all-gather(bf16[128,768]{1,0:T(8,128)(2,1)S(1)} %pad_maximum_fusion.2), channel_id=4, replica_groups=mesh['blk'=4,'grp'=8] {'blk'}, dimensions={0}, use_global_device_ids=true | all-gather | bytes 983040 | tf_op jit(solution)/shard_map/all_gather | solution.py:26
  185.9 0.6 reshape.93
  186.5 0.6 convolution_convert_fusion
  188.3 0.9 fusion
  189.1 0.9 fusion.1
  190.0 2.8 pad_maximum_fusion
  193.0 55.7 %reduce-scatter.5.cloned.1.call-done = bf16[144,2,1152]{2,0,1:T(8,128)(2,1)} async-done(((bf16[1152,2,1152]{2,0,1:T(8,128)(2,1)}), bf16[144,2,1152]{2,0,1:T(8,128)(2,1)}) %reduce-scatter.5.cloned.1.call-update) | async-done | bytes 663568 | tf_op jit(solution)/shard_map/reduce_scatter | solution.py:72
  248.7 3.5 %copy.28 = bf16[144,2,1152]{0,1,2:T(2,128)(2,1)S(1)} copy(bf16[144,2,1152]{2,0,1:T(8,128)(2,1)} %reduce-scatter.5.cloned.1.call-done) | data formatting | bytes 1327104
  252.2 1.5 reshape.107
  253.8 0.7 fusion.54
  254.5 24.0 %reduce-scatter.7.cloned.1.call-done = bf16[288,288]{1,0:T(8,128)(2,1)} async-done(((bf16[1152,288]{1,0:T(8,128)(2,1)}), bf16[288,288]{1,0:T(8,128)(2,1)}) %reduce-scatter.7.cloned.1.call-update) | async-done | bytes 165904
  278.5 1.1 reshape.108
  279.8 0.9 copy.21
  (37 shorter events, 3.8 us)
Async XLA Ops:
  7.2 1.0 copy-start
  7.2 19.3 %copy-start.4 = (s32[1,1,4]{2,1,0:T(1,128)S(1)}, s32[1,1,4]{2,1,0:T(1,128)}, u32[]{:S(2)}) copy-start(s32[1,1,4]{2,1,0:T(1,128)} %param.9) | copy-start | bytes 52
  7.2 19.7 %copy-start.2 = (bf16[1,1,4,128,128]{4,3,2,1,0:T(8,128)(2,1)S(1)}, bf16[1,1,4,128,128]{4,3,2,1,0:T(8,128)(2,1)}, u32[]{:S(2)}) copy-start(bf16[1,1,4,128,128]{4,3,2,1,0:T(8,128)(2,1)} %param.7) | copy-start | bytes 393220
  7.2 19.9 %copy-start.1 = (bf16[1,1,4,128,128]{4,3,2,1,0:T(8,128)(2,1)S(1)}, bf16[1,1,4,128,128]{4,3,2,1,0:T(8,128)(2,1)}, u32[]{:S(2)}) copy-start(bf16[1,1,4,128,128]{4,3,2,1,0:T(8,128)(2,1)} %param.8) | copy-start | bytes 393220
  7.2 241.5 %reduce-scatter.5.cloned.1.call-start = ((), (), s32[]{:S(2)}) async-start(), calls=%async_computation.2 | async-start | bytes 5971968 | tf_op jit(solution)/shard_map/reduce_scatter | solution.py:72
  146.0 41.1 %copy-start.3 = (f32[384]{0:T(512)}, f32[384]{0:T(512)S(1)}, u32[]{:S(2)}) copy-start(f32[384]{0:T(512)S(1)} %add_divide_fusion) | copy-start | bytes 4612
  192.9 85.6 %reduce-scatter.7.cloned.1.call-start = ((), (), s32[]{:S(2)}) async-start(), calls=%async_computation.3 | async-start | bytes 1105920
Sparse Core Ops, SparseCore 0:
  193.0 55.6 reduce-scatter.4
  253.9 24.5 reduce-scatter.6
